TPU v7x, 32 devices: a whole 2x2x4 slice. The times are simulated.
32 devices in a mesh: loop: 8 (over z, y), row: 4 (over x, core).
Axes of the slice: x: 2, y: 2, z: 4, core: 2. Of those that a mesh axis runs over, the one named last changes fastest.
Arguments:
- slab: float32 [2048, 16384], P('row', 'loop'), may hold values from -6 to 6
- rotations: float32 [32, 512, 512], P('loop', 'row')
- slab_pair: int32 [4], replicated, may hold values from 0 to 31, as said below
Outputs:
- moved: float32 [2048, 16384], P('row', 'loop')
Inputs may be any that keep to these rules, and one draw needn't show every extreme that they name: `slab_pair`: distinct pair numbers.
All inputs are finite; a program needn't handle non-finite values.
Results may differ from a plain program's by a relative error of at most 0.00009.
Values sent between devices are 32-bit elements; how exact they have to be, the bound alone decides.
No kernel may reach another device: no remote copies, remote signals or barrier semaphores. Data moves between devices by JAX's collectives and lax.ppermute only.
A program may use at most 64 MiB of HBM per device.

v0:
```python
import jax
import jax.numpy as jnp
from jax import lax
from jax.sharding import PartitionSpec as P


def from_behind(shard, axis, by):
    length = lax.axis_size(axis)
    pairs = [(i, i + by) for i in range(length) if 0 <= i + by < length]
    return lax.ppermute(shard, axis, pairs)


def from_root(shard, axis, root):
    mine = lax.axis_index(axis) == root
    return lax.psum(jnp.where(mine, shard, jnp.zeros_like(shard)), axis)


def left_apply(rotation, columns):
    return jnp.einsum("ij,in->jn", rotation, columns, precision=lax.Precision.HIGHEST)


def move_blocks(last_top, first_bottom):
    incoming_top = from_behind(last_top, "loop", 1)
    incoming_bottom = from_behind(first_bottom, "loop", -1)
    return (incoming_top, incoming_bottom)


def arrange(updated, incoming_top, incoming_bottom, pair_dev, half):
    rows = updated.shape[0]
    blocks = updated.reshape(rows, pair_dev, 2, half)
    tops = blocks[:, :, 0]
    bottoms = blocks[:, :, 1]
    new_tops = jnp.concatenate([incoming_top[:, None], tops[:, : pair_dev - 1]], axis=1)
    new_bottoms = jnp.concatenate([bottoms[:, 1:], incoming_bottom[:, None]], axis=1)
    place = lax.axis_index("loop") * pair_dev + jnp.arange(pair_dev, dtype=jnp.int32)
    total_pairs = pair_dev * lax.axis_size("loop")
    new_tops = jnp.where((place == 0)[None, :, None], tops, new_tops)
    new_tops = jnp.where((place == 1)[None, :, None], bottoms[:, :1], new_tops)
    new_bottoms = jnp.where(
        (place == total_pairs - 1)[None, :, None], tops[:, pair_dev - 1 :], new_bottoms
    )
    return jnp.stack([new_tops, new_bottoms], axis=2).reshape(rows, pair_dev * 2 * half)


def per_device(slab, rotations, slab_pair):
    pair_dev = rotations.shape[0]
    width = rotations.shape[2]
    half = width // 2
    rows = slab.shape[0]
    panels = slab.reshape(rows, pair_dev, width)
    wanted = slab_pair[lax.axis_index("row")]
    local_slot = wanted % pair_dev
    owner = wanted // pair_dev
    gathered = lax.all_gather(rotations, "row", axis=1, tiled=True)
    turned = jnp.einsum("rpi,pij->rpj", panels, gathered, precision=lax.Precision.HIGHEST)
    picked = lax.dynamic_index_in_dim(gathered, local_slot, 0, keepdims=False)
    rotation = from_root(picked, "loop", owner)
    flat = turned.reshape(rows, pair_dev * width)
    updated = left_apply(rotation, flat)
    last_top = updated[:, (pair_dev - 1) * width : (pair_dev - 1) * width + half]
    first_bottom = updated[:, half:width]
    incoming_top, incoming_bottom = move_blocks(last_top, first_bottom)
    return arrange(updated, incoming_top, incoming_bottom, pair_dev, half)


def solution(mesh):
    return jax.shard_map(
        per_device,
        mesh=mesh,
        in_specs=(P("row", "loop"), P("loop", "row", None), P()),
        out_specs=P("row", "loop"),
        check_vma=False,
    )
```

profile of v0, /device:TPU:0, one launch (start us, length us, event | category | flops | bytes accessed | tf_op | source)
XLA Modules:
  0.0 199.6 jit_solution(9748989037205450885)
XLA Ops:
  6.5 0.0 copy-start.1
  6.5 0.0 all-gather.2.cloned.1.call-start
  6.5 2.5 %copy.13 = f32[4,128,512]{1,2,0:T(8,128)} copy(f32[4,128,512]{2,1,0:T(8,128)} %param.4) | data formatting | bytes 2097152 | tf_op args[1]
  9.1 0.0 all-gather.2.cloned.1.call-update
  9.1 0.0 all-reduce.2.cloned.1.call-start
  9.2 0.0 copy-done.1
  9.2 0.7 dynamic_slice.7
  12.6 34.4 %all-gather.2.cloned.1.call-done = f32[4,512,512]{1,2,0:T(8,128)} async-done(((f32[4,128,512]{1,2,0:T(8,128)}), f32[4,512,512]{1,2,0:T(8,128)}) %all-gather.2.cloned.1.call-update) | async-done | bytes 4194320 | tf_op jit(solution)/shard_map/all_gather | solution.py:54
  47.0 2.3 %select_bitcast_fusion = f32[512,512]{0,1:T(8,128)} fusion(f32[4,512,512]{1,2,0:T(8,128)} %all-gather.2.cloned.1.call-done, s32[]{:T(128)S(6)} %select_n.53, pred[]{:T(512)S(6)} %eq.27), kind=kLoop, calls=%fused_computation.11 | loop fusion | flops 262144 | bytes 2097157 | tf_op jit(solution)/shard_map/jit(_where)/select_n | solution.py:15
  49.3 0.0 all-reduce.2.cloned.1.call-update
  49.4 12.0 %fusion = f32[4,512,512]{2,1,0:T(8,128)} fusion(f32[4,512,512]{1,2,0:T(8,128)} %all-gather.2.cloned.1.call-done, f32[64,4,8,512]{3,2,1,0:T(8,128)} %bitcast.36), kind=kOutput, calls=%fused_computation | convolution fusion | flops 6442450944 | bytes 12582912 | tf_op jit(solution)/shard_map/rpi,pij->rpj/dot_general | solution.py:55
  61.4 67.1 %all-reduce.2.cloned.1.call-done = f32[512,512]{0,1:T(8,128)} async-done(((f32[512,512]{0,1:T(8,128)}), f32[512,512]{0,1:T(8,128)}) %all-reduce.2.cloned.1.call-update) | async-done | bytes 1048592 | tf_op jit(solution)/shard_map/psum | solution.py:15
  128.5 9.0 %fusion.9 = f32[512,2048]{1,0:T(8,128)S(1)} fusion(f32[512,512]{0,1:T(8,128)} %all-reduce.2.cloned.1.call-done, f32[512,2048]{0,1:T(8,128)} %bitcast.30), kind=kOutput, calls=%fused_computation.20 | convolution fusion | flops 6442450944 | bytes 9437184 | tf_op jit(solution)/shard_map/ij,in->jn/dot_general | solution.py:19
  137.6 0.0 copy-start
  137.6 2.0 %copy-done = f32[512,2048]{1,0:T(8,128)} copy-done((f32[512,2048]{1,0:T(8,128)}, f32[512,2048]{1,0:T(8,128)S(1)}, u32[]{:S(2)}) %copy-start) | copy-done | bytes 4194328
  139.6 0.1 fusion.7
  139.7 6.6 %reshape.61 = f32[512,4,2,256]{3,2,1,0:T(2,128)} reshape(f32[512,2048]{1,0:T(8,128)} %copy-done) | data formatting | bytes 8388608 | tf_op jit(solution)/shard_map/reshape | solution.py:30
  146.3 7.1 %fusion.8 = (f32[512,4,1,256]{3,2,1,0:T(1,128)S(1)}, f32[512,4,1,256]{3,2,1,0:T(1,128)S(1)}) fusion(f32[512,4,2,256]{3,2,1,0:T(2,128)} %reshape.61), kind=kLoop, calls=%fused_computation.19 | loop fusion | bytes 8388608 | tf_op jit(solution)/shard_map/slice | solution.py:31
  153.3 0.4 copy.29
  153.8 0.1 slice_bitcast_fusion
  153.9 3.2 %collective-permute-start = (f32[512,256]{1,0:T(8,128)S(1)}, f32[512,256]{1,0:T(8,128)S(1)}, u32[]{:S(2)}, u32[]{:S(2)}) collective-permute-start(f32[512,256]{1,0:T(8,128)S(1)} %get-tuple-element.5), channel_id=1, source_target_pairs={{0,4},{4,8},{8,12},{12,16},{16,20},{20,24},{24,28},{1,5},{5,9},{9,... | collective-permute-start | bytes 1572872 | tf_op jit(solution)/shard_map/ppermute | solution.py:10
  157.1 1.3 collective-permute-start.1
  158.4 0.4 copy.30
  158.8 0.1 slice_bitcast_fusion.1
  159.0 13.0 %collective-permute-done.1 = f32[512,256]{1,0:T(8,128)S(1)} collective-permute-done((f32[512,256]{1,0:T(8,128)S(1)}, f32[512,256]{1,0:T(8,128)S(1)}, u32[]{:S(2)}, u32[]{:S(2)}) %collective-permute-start.1) | collective-permute-done | bytes 524320 | tf_op jit(solution)/shard_map/ppermute | solution.py:10
  172.0 0.2 maximum_select_fusion.1
  172.3 6.8 %collective-permute-done = f32[512,256]{1,0:T(8,128)S(1)} collective-permute-done((f32[512,256]{1,0:T(8,128)S(1)}, f32[512,256]{1,0:T(8,128)S(1)}, u32[]{:S(2)}, u32[]{:S(2)}) %collective-permute-start) | collective-permute-done | bytes 524320 | tf_op jit(solution)/shard_map/ppermute | solution.py:10
  179.1 0.6 fusion.3
  179.7 2.5 %pad_maximum_fusion = f32[512,4,2,256]{3,0,2,1:T(8,128)} fusion(f32[512,4,1,256]{3,0,2,1:T(8,128)S(1)} %maximum_select_fusion.1, f32[512,4,1,256]{3,0,2,1:T(8,128)S(1)} %fusion.3), kind=kLoop, calls=%fused_computation.3 | loop fusion | flops 1048576 | bytes 8388608 | tf_op jit(solution)/shard_map/stack | solution.py:42
  182.2 5.2 %copy.17 = f32[512,4,2,256]{0,3,2,1:T(8,128)} copy(f32[512,4,2,256]{3,0,2,1:T(8,128)} %pad_maximum_fusion) | data formatting | bytes 8388608 | tf_op jit(solution)/shard_map/stack | solution.py:42
  187.4 5.3 %copy.18 = f32[512,2048]{1,0:T(8,128)} copy(f32[512,2048]{0,1:T(8,128)} %bitcast.31) | data formatting | bytes 8388608 | tf_op jit(solution)/shard_map/reshape | solution.py:42
  (4 shorter events, 0.1 us)
Async XLA Ops:
  6.5 2.6 %copy-start.1 = (s32[4]{0:T(128)S(1)}, s32[4]{0:T(128)}, u32[]{:S(2)}) copy-start(s32[4]{0:T(128)} %param.5) | copy-start | bytes 52
  6.5 40.4 %all-gather.2.cloned.1.call-start = ((), (), s32[]{:S(2)}) async-start(), calls=%async_computation | async-start | bytes 5242880 | tf_op jit(solution)/shard_map/all_gather | solution.py:54
  9.1 119.4 %all-reduce.2.cloned.1.call-start = ((), (), s32[]{:S(2)}) async-start(), calls=%async_computation.1 | async-start | bytes 2097152 | tf_op jit(solution)/shard_map/psum | solution.py:15
  137.6 2.0 %copy-start = (f32[512,2048]{1,0:T(8,128)}, f32[512,2048]{1,0:T(8,128)S(1)}, u32[]{:S(2)}) copy-start(f32[512,2048]{1,0:T(8,128)S(1)} %fusion.9) | copy-start | bytes 12582916
  153.9 25.2 %collective-permute-start = (f32[512,256]{1,0:T(8,128)S(1)}, f32[512,256]{1,0:T(8,128)S(1)}, u32[]{:S(2)}, u32[]{:S(2)}) collective-permute-start(f32[512,256]{1,0:T(8,128)S(1)} %get-tuple-element.5), channel_id=1, source_target_pairs={{0,4},{4,8},{8,12},{12,16},{16,20},{20,24},{24,28},{1,5},{5,9},{9,... | collective-permute-start | bytes 1572872 | tf_op jit(solution)/shard_map/ppermute | solution.py:10
  157.1 14.9 %collective-permute-start.1 = (f32[512,256]{1,0:T(8,128)S(1)}, f32[512,256]{1,0:T(8,128)S(1)}, u32[]{:S(2)}, u32[]{:S(2)}) collective-permute-start(f32[512,256]{1,0:T(8,128)S(1)} %get-tuple-element.6), channel_id=1, source_target_pairs={{4,0},{8,4},{12,8},{16,12},{20,16},{24,20},{28,24},{5,1},{9,5},{13... | collective-permute-start | bytes 1572872 | tf_op jit(solution)/shard_map/ppermute | solution.py:10
Sparse Core Ops, SparseCore 0:
  9.2 37.7 all-gather.1
  50.5 77.9 all-reduce.1
where the time goes:
time: 200 us
  waiting for transfers between devices  121 us (60%)
  local copies, waits for them, and re-layouts  30.6 us (15%)
  matrix products  21.1 us (11%)
  between operations  16.3 us (8%)
  other arithmetic  5.63 us (3%)
  starting transfers between devices  4.53 us (2%)
    psum x1, waiting for transfers between devices, from_root(): return lax.psum(jnp.where(mine, shard, jnp.zeros_like(shard)), axis)  67.1 us
    all_gather x1, waiting for transfers between devices, per_device(): gathered = lax.all_gather(rotations, 'row', axis=1, tiled=True)  34.4 us
    ppermute x2, waiting for transfers between devices, from_behind(): return lax.ppermute(shard, axis, pairs)  19.9 us
    dot_general x1, matrix products, per_device(): jnp.einsum('rpi,pij->rpj', panels, gathered, precision=lax.Precision.HIGH...  12 us
    dot_general x1, matrix products, left_apply(): jnp.einsum('ij,in->jn', rotation, columns, precision=lax.Precision.HIGHEST)  9.04 us
    slice x1, local copies, waits for them, and re-layouts, arrange(): tops = blocks[:, :, 0]  7.06 us
    reshape x1, local copies, waits for them, and re-layouts, arrange(): blocks = updated.reshape(rows, pair_dev, 2, half)  6.59 us
    unnamed x7, local copies, waits for them, and re-layouts  5.36 us
  transfers between devices with their start and end apart: 4, of which 4 were waited for; matrix products, arithmetic and copies ran while one was open for 7% of the time, Pallas kernels for 0%

commit v1 on v0

--- a/solution.py
+++ b/solution.py
@@ -2,6 +2,11 @@
 import jax.numpy as jnp
 from jax import lax
 from jax.sharding import PartitionSpec as P
+
+
+def fit_trails(target, device_axis):
+    row_out = lax.all_gather(target, device_axis).sum(axis=0)
+    return row_out
 
 
 def from_behind(shard, axis, by):
@@ -12,7 +17,7 @@
 
 def from_root(shard, axis, root):
     mine = lax.axis_index(axis) == root
-    return lax.psum(jnp.where(mine, shard, jnp.zeros_like(shard)), axis)
+    return fit_trails(jnp.where(mine, shard, jnp.zeros_like(shard)), axis)
 
 
 def left_apply(rotation, columns):

time: 200 us -> 250 us (1.25)
  waiting for transfers between devices: 121 us -> 159 us
  matrix products: 21.1 us -> 27.1 us
  other arithmetic: 5.63 us -> 9.11 us
    all_gather x0 -> x1, waiting for transfers between devices: none -> 113 us  [fit_trails(): row_out = lax.all_gather(target, device_axis).sum(axis=0)]
    psum x1 -> x0, waiting for transfers between devices: 67.1 us -> none  [from_root(): return lax.psum(jnp.where(mine, shard, jnp.zeros_like(shard)), axis)]
    ppermute x2, waiting for transfers between devices: 19.9 us -> 11 us  [from_behind(): return lax.ppermute(shard, axis, pairs)]
    dot_general x1, matrix products: 9.04 us -> 15.1 us  [left_apply(): jnp.einsum('ij,in->jn', rotation, columns, precision=lax.Precision.HIGHEST)]
    unnamed x0 -> x1, other arithmetic: none -> 4.49 us
  transfers between devices with their start and end apart: 4 -> 4, of which waited for: 4 -> 4; matrix products, arithmetic and copies ran while one was open for 7% -> 8% of each run, Pallas kernels for 0% -> 0%
where the time goes in v1:
time: 250 us; the launch traced here: 249 us
  waiting for transfers between devices  159 us (64%)
  local copies, waits for them, and re-layouts  32.1 us (13%)
  matrix products  27.1 us (11%)
  between operations  16.1 us (6%)
  other arithmetic  9.11 us (4%)
  starting transfers between devices  5.9 us (2%)
    all_gather x1, waiting for transfers between devices, fit_trails(): row_out = lax.all_gather(target, device_axis).sum(axis=0)  113 us
    all_gather x1, waiting for transfers between devices, per_device(): gathered = lax.all_gather(rotations, 'row', axis=1, tiled=True)  34.6 us
    dot_general x1, matrix products, left_apply(): jnp.einsum('ij,in->jn', rotation, columns, precision=lax.Precision.HIGHEST)  15.1 us
    dot_general x1, matrix products, per_device(): jnp.einsum('rpi,pij->rpj', panels, gathered, precision=lax.Precision.HIGH...  12 us
    ppermute x2, waiting for transfers between devices, from_behind(): return lax.ppermute(shard, axis, pairs)  11 us
    slice x1, local copies, waits for them, and re-layouts, arrange(): tops = blocks[:, :, 0]  7.06 us
    reshape x1, local copies, waits for them, and re-layouts, arrange(): blocks = updated.reshape(rows, pair_dev, 2, half)  6.77 us
    ppermute x2, starting transfers between devices, from_behind(): return lax.ppermute(shard, axis, pairs)  5.86 us
  transfers between devices with their start and end apart: 4, of which 4 were waited for; matrix products, arithmetic and copies ran while one was open for 8% of the time, Pallas kernels for 0%

profile of v1, /device:TPU:0, one launch (start us, length us, event | category | flops | bytes accessed | tf_op | source)
XLA Modules:
  0.0 249.1 jit_solution(6507099863333137205)
XLA Ops:
  6.5 0.0 copy-start.1
  6.5 0.0 all-gather.3.cloned.1.call-start
  6.5 2.5 %copy.19 = f32[4,128,512]{1,2,0:T(8,128)} copy(f32[4,128,512]{2,1,0:T(8,128)} %param.4) | data formatting | bytes 2097152 | tf_op args[1]
  9.1 0.0 all-gather.3.cloned.1.call-update
  9.1 0.0 all-gather.5.cloned.1.call-start
  9.2 0.0 copy-done.1
  9.2 0.6 dynamic_slice.7
  12.4 34.6 %all-gather.3.cloned.1.call-done = f32[4,512,512]{1,2,0:T(8,128)} async-done(((f32[4,128,512]{1,2,0:T(8,128)}), f32[4,512,512]{1,2,0:T(8,128)}) %all-gather.3.cloned.1.call-update) | async-done | bytes 4194320 | tf_op jit(solution)/shard_map/all_gather | solution.py:59
  47.0 1.3 dynamic-slice_select_fusion
  48.3 1.4 copy.20
  49.7 0.0 all-gather.5.cloned.1.call-update
  49.7 12.0 %fusion = f32[4,512,512]{2,1,0:T(8,128)} fusion(f32[4,512,512]{1,2,0:T(8,128)} %all-gather.3.cloned.1.call-done, f32[64,4,8,512]{3,2,1,0:T(8,128)} %bitcast.34), kind=kOutput, calls=%fused_computation | convolution fusion | flops 6442450944 | bytes 12582912 | tf_op jit(solution)/shard_map/rpi,pij->rpj/dot_general | solution.py:60
  61.8 113.0 %all-gather.5.cloned.1.call-done = f32[8,512,512]{2,1,0:T(8,128)} async-done(((f32[1,512,512]{2,1,0:T(8,128)}), f32[8,512,512]{2,1,0:T(8,128)}) %all-gather.5.cloned.1.call-update) | async-done | bytes 8388624 | tf_op jit(solution)/shard_map/all_gather | solution.py:8
  174.8 4.5 %reduce_sum.9 = f32[512,512]{1,0:T(8,128)S(1)} reduce(f32[8,512,512]{2,1,0:T(8,128)} %all-gather.5.cloned.1.call-done, f32[]{:T(128)} %constant.45.clone.1), dimensions={0}, to_apply=%region_0.1 | reduce | flops 1835008 | bytes 9437188
  179.3 15.1 %fusion.9 = f32[512,2048]{1,0:T(8,128)S(1)} fusion(f32[512,512]{1,0:T(8,128)S(1)} %reduce_sum.9, f32[512,2048]{0,1:T(8,128)} %bitcast.28), kind=kOutput, calls=%fused_computation.20 | convolution fusion | flops 6442450944 | bytes 9437184 | tf_op jit(solution)/shard_map/ij,in->jn/dot_general | solution.py:24
  194.4 0.0 copy-start
  194.4 2.0 copy-done
  196.4 0.1 fusion.7
  196.5 6.8 %reshape.58 = f32[512,4,2,256]{3,2,1,0:T(2,128)} reshape(f32[512,2048]{1,0:T(8,128)} %copy-done) | data formatting | bytes 8388608 | tf_op jit(solution)/shard_map/reshape | solution.py:35
  203.3 1.3 collective-permute-start.1
  204.6 7.1 %fusion.8 = (f32[512,4,1,256]{3,2,1,0:T(1,128)S(1)}, f32[512,4,1,256]{3,2,1,0:T(1,128)S(1)}) fusion(f32[512,4,2,256]{3,2,1,0:T(2,128)} %reshape.58), kind=kLoop, calls=%fused_computation.19 | loop fusion | bytes 8388608 | tf_op jit(solution)/shard_map/slice | solution.py:36
  211.6 0.4 copy.38
  212.1 0.1 slice_bitcast_fusion
  212.2 0.4 copy.39
  212.6 0.1 slice_bitcast_fusion.1
  212.7 4.6 %collective-permute-start = (f32[512,256]{1,0:T(8,128)S(1)}, f32[512,256]{1,0:T(8,128)S(1)}, u32[]{:S(2)}, u32[]{:S(2)}) collective-permute-start(f32[512,256]{1,0:T(8,128)S(1)} %get-tuple-element.5), channel_id=1, source_target_pairs={{0,4},{4,8},{8,12},{12,16},{16,20},{20,24},{24,28},{1,5},{5,9},{9,... | collective-permute-start | bytes 1572872 | tf_op jit(solution)/shard_map/ppermute | solution.py:15
  217.4 1.1 collective-permute-done.1
  218.4 0.2 maximum_select_fusion.1
  218.7 10.0 %collective-permute-done = f32[512,256]{1,0:T(8,128)S(1)} collective-permute-done((f32[512,256]{1,0:T(8,128)S(1)}, f32[512,256]{1,0:T(8,128)S(1)}, u32[]{:S(2)}, u32[]{:S(2)}) %collective-permute-start) | collective-permute-done | bytes 524320 | tf_op jit(solution)/shard_map/ppermute | solution.py:15
  228.6 0.6 fusion.3
  229.2 2.5 pad_maximum_fusion
  231.7 5.2 %copy.25 = f32[512,4,2,256]{0,3,2,1:T(8,128)} copy(f32[512,4,2,256]{3,0,2,1:T(8,128)} %pad_maximum_fusion) | data formatting | bytes 8388608 | tf_op jit(solution)/shard_map/stack | solution.py:47
  236.9 5.3 %copy.26 = f32[512,2048]{1,0:T(8,128)} copy(f32[512,2048]{0,1:T(8,128)} %bitcast.29) | data formatting | bytes 8388608 | tf_op jit(solution)/shard_map/reshape | solution.py:47
  (4 shorter events, 0.1 us)
Async XLA Ops:
  6.5 2.6 %copy-start.1 = (s32[4]{0:T(128)S(1)}, s32[4]{0:T(128)}, u32[]{:S(2)}) copy-start(s32[4]{0:T(128)} %param.5) | copy-start | bytes 52
  6.5 40.4 %all-gather.3.cloned.1.call-start = ((), (), s32[]{:S(2)}) async-start(), calls=%async_computation | async-start | bytes 5242880 | tf_op jit(solution)/shard_map/all_gather | solution.py:59
  9.1 165.7 %all-gather.5.cloned.1.call-start = ((), (), s32[]{:S(2)}) async-start(), calls=%async_computation.1 | async-start | bytes 9437184 | tf_op jit(solution)/shard_map/all_gather | solution.py:8
  194.4 2.0 copy-start
  203.3 15.1 %collective-permute-start.1 = (f32[512,256]{1,0:T(8,128)S(1)}, f32[512,256]{1,0:T(8,128)S(1)}, u32[]{:S(2)}, u32[]{:S(2)}) collective-permute-start(f32[512,256]{1,0:T(8,128)S(1)} %get-tuple-element.6), channel_id=1, source_target_pairs={{4,0},{8,4},{12,8},{16,12},{20,16},{24,20},{28,24},{5,1},{9,5},{13... | collective-permute-start | bytes 1572872 | tf_op jit(solution)/shard_map/ppermute | solution.py:15
  212.7 15.9 %collective-permute-start = (f32[512,256]{1,0:T(8,128)S(1)}, f32[512,256]{1,0:T(8,128)S(1)}, u32[]{:S(2)}, u32[]{:S(2)}) collective-permute-start(f32[512,256]{1,0:T(8,128)S(1)} %get-tuple-element.5), channel_id=1, source_target_pairs={{0,4},{4,8},{8,12},{12,16},{16,20},{20,24},{24,28},{1,5},{5,9},{9,... | collective-permute-start | bytes 1572872 | tf_op jit(solution)/shard_map/ppermute | solution.py:15
Sparse Core Ops, SparseCore 0:
  9.2 37.7 all-gather.2
  49.8 124.9 all-gather.4
